TPU v7x, 512 devices: a whole 4x8x8 slice. The times are simulated.
512 devices in a mesh: section: 8 (over x, core), replica: 64 (over z, y).
Axes of the slice: x: 4, y: 8, z: 8, core: 2. Of those that a mesh axis runs over, the one named last changes fastest.
Arguments:
- pending_section_entries: bfloat16 [8, 128, 14, 14, 512], P('section', 'replica'), may hold values from -40 to 40
- arriving_microsets: bfloat16 [1, 128, 14, 14, 512], P(None, 'replica'), may hold values from -40 to 40
- opening_filter_kernel: bfloat16 [8, 3, 3, 512, 512], P('section'), may hold values from -0.09375 to 0.09375
- closing_filter_kernel: bfloat16 [8, 3, 3, 512, 512], P('section'), may hold values from -0.09375 to 0.09375
- stretch_factors: float32 [8, 2, 512], P('section'), may hold values from 0.5 to 1.5
- shift_terms: float32 [8, 2, 512], P('section'), may hold values from -3 to 3
Outputs:
- produced: bfloat16 [8, 2, 128, 14, 14, 512], P('section', None, 'replica')
All inputs are finite; a program needn't handle non-finite values.
Results may differ from a plain program's by a relative error of at most 0.0084.
Values may be sent and summed in bfloat16 or wider, within the bound.
No kernel may reach another device: no remote copies, remote signals or barrier semaphores. Data moves between devices by JAX's collectives and lax.ppermute only.
A program may use at most 64 MiB of HBM per device.

v0:
```python
import jax
import jax.numpy as jnp
from jax import lax
from jax.sharding import PartitionSpec as P

TICKS = 2


def from_behind(shard, axis, by):
    length = lax.axis_size(axis)
    pairs = [(i, i + by) for i in range(length) if 0 <= i + by < length]
    return lax.ppermute(shard, axis, pairs)


def convolve(maps, kernel):
    return lax.conv_general_dilated(
        maps,
        kernel,
        (1, 1),
        "SAME",
        dimension_numbers=("NHWC", "HWIO", "NHWC"),
        preferred_element_type=jnp.float32,
    )


def batch_statistics(conv_out, replica_total):
    summed = lax.psum(jnp.sum(conv_out, axis=(0, 1, 2)), "replica")
    mean = summed / replica_total
    centred = conv_out - mean
    spread = lax.psum(jnp.sum(centred * centred, axis=(0, 1, 2)), "replica")
    var = spread / replica_total
    return (mean, var)


def coefficients(conv_out, gain, bias, replica_total):
    mean, var = batch_statistics(conv_out, replica_total)
    scale = gain * lax.rsqrt(var + 1e-05)
    return (scale, bias - mean * scale)


def store(conv_out):
    return lax.optimization_barrier(conv_out.astype(jnp.bfloat16))


def normalize(stored, scale, offset):
    return jnp.maximum(stored.astype(jnp.float32) * scale + offset, 0.0).astype(jnp.bfloat16)


def body(
    pending_section_entries,
    arriving_microsets,
    opening_filter_kernel,
    closing_filter_kernel,
    stretch_factors,
    shift_terms,
):
    replica_total = (
        lax.axis_size("replica")
        * pending_section_entries.shape[1]
        * pending_section_entries.shape[2]
        * pending_section_entries.shape[3]
    )
    is_first = lax.axis_index("section") == 0
    first_kernel = opening_filter_kernel[0]
    second_kernel = closing_filter_kernel[0]
    current_feature_map = pending_section_entries[0]
    results = []
    for tick in range(TICKS):
        conv_one = convolve(current_feature_map, first_kernel)
        scale_one, offset_one = coefficients(
            conv_one, stretch_factors[0, 0], shift_terms[0, 0], replica_total
        )
        hidden = normalize(store(conv_one), scale_one, offset_one)
        conv_two = convolve(hidden, second_kernel)
        stored_two = store(conv_two)
        last = tick + 1 == TICKS
        scale_two, offset_two = coefficients(
            conv_two, stretch_factors[0, 1], shift_terms[0, 1], replica_total
        )
        output = normalize(stored_two, scale_two, offset_two)
        if not last:
            moved = from_behind(output, "section", 1)
        results.append(output)
        if not last:
            current_feature_map = jnp.where(is_first, arriving_microsets[tick], moved)
    return jnp.stack(results, axis=0)[None]


def solution(mesh):
    in_specs = (
        P("section", "replica", None, None, None),
        P(None, "replica", None, None, None),
        P("section", None, None, None, None),
        P("section", None, None, None, None),
        P("section", None, None),
        P("section", None, None),
    )
    out_specs = P("section", None, "replica", None, None, None)
    return jax.shard_map(body, mesh=mesh, in_specs=in_specs, out_specs=out_specs, check_vma=False)
```

profile of v0, /device:TPU:10, one launch (start us, length us, event | category | flops | bytes accessed | tf_op | source)
XLA Modules:
  0.0 1161.6 jit_solution(2862424807309763926)
XLA Ops:
  0.0 0.8 fusion.68
  0.8 0.8 fusion.69
  1.5 1.4 pad
  3.0 0.1 copy.16
  3.1 0.1 slice.28
  3.2 4.6 select_reduce_fusion.7
  7.8 146.3 %psum.56 = f32[512]{0:T(512)S(1)} all-reduce(f32[512]{0:T(512)S(1)} %get-tuple-element.25), channel_id=1, replica_groups=mesh['section'=8,'replica'=64] {'replica'}, use_global_device_ids=true, to_apply=%region_1.0 | all-reduce | flops 512 | bytes 4096 | tf_op jit(solution)/shard_map/psum | solution.py:27
  154.2 0.2 select_reduce_fusion.6
  154.4 141.9 %psum.57 = f32[512]{0:T(512)S(1)} all-reduce(f32[512]{0:T(512)S(1)} %get-tuple-element.19), channel_id=1, replica_groups=mesh['section'=8,'replica'=64] {'replica'}, use_global_device_ids=true, to_apply=%region_3.0 | all-reduce | flops 512 | bytes 4096 | tf_op jit(solution)/shard_map/psum | solution.py:30
  296.4 0.5 copy.17
  296.9 0.2 reshape.18
  297.1 0.1 fusion.48
  297.2 0.1 pad.2
  297.4 0.2 reshape.23
  297.6 0.1 slice.30
  297.8 4.6 select_reduce_fusion.5
  302.4 138.0 %psum.58 = f32[512]{0:T(512)S(1)} all-reduce(f32[512]{0:T(512)S(1)} %get-tuple-element.27), channel_id=1, replica_groups=mesh['section'=8,'replica'=64] {'replica'}, use_global_device_ids=true, to_apply=%region_5.0 | all-reduce | flops 512 | bytes 4096 | tf_op jit(solution)/shard_map/psum | solution.py:27
  440.4 0.2 select_reduce_fusion.4
  440.6 140.0 %psum.59 = f32[512]{0:T(512)S(1)} all-reduce(f32[512]{0:T(512)S(1)} %get-tuple-element.17), channel_id=1, replica_groups=mesh['section'=8,'replica'=64] {'replica'}, use_global_device_ids=true, to_apply=%region_7.0 | all-reduce | flops 512 | bytes 4096 | tf_op jit(solution)/shard_map/psum | solution.py:30
  580.6 0.5 copy.20
  581.1 0.2 reshape.27
  581.3 0.1 maximum_convert_fusion.2
  581.5 1.9 collective-permute-start
  583.4 0.1 fusion.70
  583.6 7.7 collective-permute-done
  591.3 0.1 pad.4
  591.5 0.2 reshape.32
  591.7 0.1 copy.23
  591.7 0.1 slice.32
  591.9 4.6 select_reduce_fusion.3
  596.5 138.0 %psum.60 = f32[512]{0:T(512)S(1)} all-reduce(f32[512]{0:T(512)S(1)} %get-tuple-element.29), channel_id=1, replica_groups=mesh['section'=8,'replica'=64] {'replica'}, use_global_device_ids=true, to_apply=%region_9.10 | all-reduce | flops 512 | bytes 4096 | tf_op jit(solution)/shard_map/psum | solution.py:27
  734.5 0.2 select_reduce_fusion.2
  734.7 140.0 %psum.61 = f32[512]{0:T(512)S(1)} all-reduce(f32[512]{0:T(512)S(1)} %get-tuple-element.15), channel_id=1, replica_groups=mesh['section'=8,'replica'=64] {'replica'}, use_global_device_ids=true, to_apply=%region_11.12 | all-reduce | flops 512 | bytes 4096 | tf_op jit(solution)/shard_map/psum | solution.py:30
  874.7 0.5 copy.24
  875.2 0.2 reshape.36
  875.4 0.1 fusion.49
  875.5 0.1 pad.6
  875.7 0.2 reshape.41
  876.0 0.1 slice.34
  876.1 4.6 select_reduce_fusion.1
  880.7 138.0 %psum.62 = f32[512]{0:T(512)S(1)} all-reduce(f32[512]{0:T(512)S(1)} %get-tuple-element.31), channel_id=1, replica_groups=mesh['section'=8,'replica'=64] {'replica'}, use_global_device_ids=true, to_apply=%region_13.14 | all-reduce | flops 512 | bytes 4096 | tf_op jit(solution)/shard_map/psum | solution.py:27
  1018.7 0.2 select_reduce_fusion
  1018.9 140.0 %psum.63 = f32[512]{0:T(512)S(1)} all-reduce(f32[512]{0:T(512)S(1)} %get-tuple-element.13), channel_id=1, replica_groups=mesh['section'=8,'replica'=64] {'replica'}, use_global_device_ids=true, to_apply=%region_15.16 | all-reduce | flops 512 | bytes 4096 | tf_op jit(solution)/shard_map/psum | solution.py:30
  1158.9 0.5 copy.27
  1159.4 0.2 reshape.45
  1159.6 0.1 fusion.50
  1159.8 0.1 maximum_bitcast_fusion
  1159.9 1.7 copy.28
  (19 shorter events, 0.4 us)
Async XLA Ops:
  0.0 3.2 copy-start.1
  581.1 10.2 copy-start
  581.5 9.8 collective-permute-start
where the time goes:
time: 1160 us
  blocking collectives  1120 us (97%)
  matrix products  18.6 us (2%)
    psum x4, blocking collectives, batch_statistics(): spread = lax.psum(jnp.sum(centred * centred, axis=(0, 1, 2)), 'replica')  562 us
    psum x4, blocking collectives, batch_statistics(): summed = lax.psum(jnp.sum(conv_out, axis=(0, 1, 2)), 'replica')  560 us
  transfers between devices with their start and end apart: 1, of which 1 were waited for; matrix products, arithmetic and copies ran while one was open for 0% of the time, Pallas kernels for 0%

commit v1 on v0

--- a/solution.py
+++ b/solution.py
@@ -24,7 +24,7 @@
 
 
 def batch_statistics(conv_out, replica_total):
-    summed = lax.psum(jnp.sum(conv_out, axis=(0, 1, 2)), "replica")
+    summed = jnp.sum(lax.all_gather(jnp.sum(conv_out, axis=(0, 1, 2)), "replica"), axis=0)
     mean = summed / replica_total
     centred = conv_out - mean
     spread = lax.psum(jnp.sum(centred * centred, axis=(0, 1, 2)), "replica")

time: 1160 us -> 797 us (0.69)
  the two profiles are of different devices: /device:TPU:10 before, /device:TPU:4 now
where the time goes in v1:
time: 797 us; the launch traced here: 796 us
  blocking collectives  756 us (95%)
  matrix products  18.6 us (2%)
  local copies, waits for them, and re-layouts  9.11 us (1%)
    psum x4, blocking collectives, batch_statistics(): spread = lax.psum(jnp.sum(centred * centred, axis=(0, 1, 2)), 'replica')  563 us
    all_gather x4, blocking collectives, batch_statistics(): lax.all_gather(jnp.sum(conv_out, axis=(0, 1, 2)), 'replica')  194 us
    conv_general_dilated x4, matrix products, convolve(): lax.conv_general_dilated(maps, kernel, (1, 1), 'SAME', dimension_numbers=...  18.6 us
  transfers between devices with their start and end apart: 1, of which 1 were waited for; matrix products, arithmetic and copies ran while one was open for 0% of the time, Pallas kernels for 0%

profile of v1, /device:TPU:4, one launch (start us, length us, event | category | flops | bytes accessed | tf_op | source)
XLA Modules:
  0.0 796.1 jit_solution(5633133422505254675)
XLA Ops:
  0.0 0.8 fusion.68
  0.8 0.8 fusion.69
  1.5 1.4 pad
  3.1 0.1 slice.28
  3.2 4.6 select_reduce_fusion.7
  7.8 56.3 %all-gather.4 = f32[64,1,512]{2,1,0:T(1,128)S(1)} all-gather(f32[1,1,512]{2,1,0:T(1,128)S(1)} %bitcast.98), channel_id=2, replica_groups=mesh['section'=8,'replica'=64] {'replica'}, dimensions={0}, use_global_device_ids=true | all-gather | bytes 133120 | tf_op jit(solution)/shard_map/all_gather | solution.py:27
  64.2 0.1 reduce_sum.109
  64.3 0.2 select_reduce_fusion.6
  64.5 140.6 %psum.28 = f32[512]{0:T(512)S(1)} all-reduce(f32[512]{0:T(512)S(1)} %get-tuple-element.19), channel_id=1, replica_groups=mesh['section'=8,'replica'=64] {'replica'}, use_global_device_ids=true, to_apply=%region_3.0 | all-reduce | flops 512 | bytes 4096 | tf_op jit(solution)/shard_map/psum | solution.py:30
  205.1 0.5 copy.31
  205.6 0.2 reshape.26
  205.9 0.1 fusion.48
  206.0 0.1 pad.2
  206.2 0.2 reshape.31
  206.4 0.1 slice.30
  206.5 4.6 select_reduce_fusion.5
  211.2 45.7 %all-gather.5 = f32[64,1,512]{2,1,0:T(1,128)S(1)} all-gather(f32[1,1,512]{2,1,0:T(1,128)S(1)} %bitcast.99), channel_id=3, replica_groups=mesh['section'=8,'replica'=64] {'replica'}, dimensions={0}, use_global_device_ids=true | all-gather | bytes 133120 | tf_op jit(solution)/shard_map/all_gather | solution.py:27
  256.9 0.1 reduce_sum.112
  257.0 0.2 select_reduce_fusion.4
  257.2 140.6 %psum.29 = f32[512]{0:T(512)S(1)} all-reduce(f32[512]{0:T(512)S(1)} %get-tuple-element.17), channel_id=1, replica_groups=mesh['section'=8,'replica'=64] {'replica'}, use_global_device_ids=true, to_apply=%region_7.0 | all-reduce | flops 512 | bytes 4096 | tf_op jit(solution)/shard_map/psum | solution.py:30
  397.8 0.5 copy.34
  398.3 0.2 reshape.35
  398.6 0.1 maximum_convert_fusion.2
  398.7 1.9 collective-permute-start
  400.7 0.1 fusion.70
  400.8 7.7 collective-permute-done
  408.6 0.1 pad.4
  408.7 0.2 reshape.40
  409.1 4.7 select_reduce_fusion.3
  413.8 45.7 %all-gather.6 = f32[64,1,512]{2,1,0:T(1,128)S(1)} all-gather(f32[1,1,512]{2,1,0:T(1,128)S(1)} %bitcast.100), channel_id=4, replica_groups=mesh['section'=8,'replica'=64] {'replica'}, dimensions={0}, use_global_device_ids=true | all-gather | bytes 133120 | tf_op jit(solution)/shard_map/all_gather | solution.py:27
  459.4 0.1 reduce_sum.115
  459.6 0.2 select_reduce_fusion.2
  459.8 140.7 %psum.30 = f32[512]{0:T(512)S(1)} all-reduce(f32[512]{0:T(512)S(1)} %get-tuple-element.15), channel_id=1, replica_groups=mesh['section'=8,'replica'=64] {'replica'}, use_global_device_ids=true, to_apply=%region_11.12 | all-reduce | flops 512 | bytes 4096 | tf_op jit(solution)/shard_map/psum | solution.py:30
  600.5 0.5 copy.38
  601.0 0.2 reshape.44
  601.2 0.1 fusion.49
  601.3 0.1 pad.6
  601.5 0.2 reshape.49
  601.9 4.7 select_reduce_fusion.1
  606.5 45.9 %all-gather.7 = f32[64,1,512]{2,1,0:T(1,128)S(1)} all-gather(f32[1,1,512]{2,1,0:T(1,128)S(1)} %bitcast.101), channel_id=5, replica_groups=mesh['section'=8,'replica'=64] {'replica'}, dimensions={0}, use_global_device_ids=true | all-gather | bytes 133120 | tf_op jit(solution)/shard_map/all_gather | solution.py:27
  652.4 0.1 reduce_sum.118
  652.5 0.2 select_reduce_fusion
  652.7 140.6 %psum.31 = f32[512]{0:T(512)S(1)} all-reduce(f32[512]{0:T(512)S(1)} %get-tuple-element.13), channel_id=1, replica_groups=mesh['section'=8,'replica'=64] {'replica'}, use_global_device_ids=true, to_apply=%region_15.16 | all-reduce | flops 512 | bytes 4096 | tf_op jit(solution)/shard_map/psum | solution.py:30
  793.4 0.5 copy.41
  793.9 0.2 reshape.53
  794.1 0.1 fusion.50
  794.2 0.1 maximum_bitcast_fusion
  794.4 1.7 copy.42
  (23 shorter events, 0.8 us)
Async XLA Ops:
  0.0 3.2 copy-start.1
  398.3 10.2 %copy-start = (bf16[1,2,14,14,512]{4,1,3,2,0:T(2,128)(2,1)S(1)}, bf16[1,2,14,14,512]{4,1,3,2,0:T(2,128)(2,1)}, u32[]{:S(2)}) copy-start(bf16[1,2,14,14,512]{4,1,3,2,0:T(2,128)(2,1)} %param.7) | copy-start | bytes 1204228
  398.7 9.8 %collective-permute-start = (bf16[2,14,14,512]{3,2,0,1:T(8,128)(2,1)S(1)}, bf16[2,14,14,512]{3,2,0,1:T(8,128)(2,1)S(1)}, u32[]{:S(2)}, u32[]{:S(2)}) collective-permute-start(bf16[2,14,14,512]{3,2,0,1:T(8,128)(2,1)S(1)} %maximum_convert_fusion.2), channel_id=1, source_target_pairs={{0,64},{64,128},{128,192},{192,256},{256,320},{320,384},{384,448},... | collective-permute-start | bytes 1204232 | tf_op jit(solution)/shard_map/ppermute | solution.py:12
